TPU v7x, 256 devices: a whole 4x4x8 slice. The times are simulated.
256 devices in a mesh: side: 2 (over x_lo), grp: 8 (over z), blk: 16 (over y, x_hi, core).
Axes of the slice: x: 4 (x_hi: 2, x_lo: 2; x = x_hi * 2 + x_lo), y: 4, z: 8, core: 2. Of those that a mesh axis runs over, the one named last changes fastest.
Arguments:
- embed_codes: bfloat16 [2, 65536, 128], P('side', ('grp', 'blk')), may hold values from -4 to 4
- embed_exps: int32 [2, 512], P('side', ('grp', 'blk')), may hold values from -1 to 1
- degrees: int32 [2, 65536], P('side', ('grp', 'blk')), may hold values from 16 to 128
- adjacency: bfloat16 [2, 49152, 128, 128], P('side', ('grp', 'blk')), may hold values from 0 to 1
- block_index: int32 [2, 2, 49152], P('side', None, ('grp', 'blk')), may hold values from 0 to 64, as said below
Outputs:
- layer_rows: bfloat16 [2, 65536, 128], P('side', ('grp', 'blk'))
Inputs may be any that keep to these rules, and one draw needn't show every extreme that they name: `block_index`: each device's list of 384 slots: its used slots come first, in non-decreasing source tile (row 1 below 64), with distinct (destination, source) pairs and destination tiles below 32; the remaining slots have source 64 and destination 0. Every list uses 384 // 4 slots or more, and in each section one list uses all 384.
All inputs are finite; a program needn't handle non-finite values.
Results may differ from a plain program's by a relative error of at most 0.0048.
Values may be sent and summed in bfloat16 or wider, within the bound.
A program may use at most 128 MiB of HBM per device.

v0:
```python
import jax
import jax.numpy as jnp
from jax import lax
from jax.sharding import PartitionSpec as P


def swapped(value, axis, stride):
    mask = 2**stride
    pairs = [(source, source ^ mask) for source in range(lax.axis_size(axis))]
    return lax.ppermute(value, axis, pairs)


def scale_rows(codes_part, exps_part, degree_part, tile_rows):
    scale = jnp.repeat(jnp.exp2(exps_part.astype(jnp.float32)), tile_rows, axis=1)
    inverse = lax.rsqrt(degree_part.astype(jnp.float32))
    return (codes_part.astype(jnp.float32) * scale[..., None] * inverse[..., None]).astype(
        jnp.bfloat16
    )


def shards(embed_codes, embed_exps, degrees, adjacency, block_index):
    tile_rows = adjacency.shape[2]
    row_width = embed_codes.shape[2]
    row_count = embed_codes.shape[1]
    tiles_dev = row_count // tile_rows
    groups = lax.axis_size("grp")
    dest_tiles = groups * tiles_dev
    capacity = adjacency.shape[1]
    other_codes, other_exps, other_degrees = swapped((embed_codes, embed_exps, degrees), "side", 0)
    source = scale_rows(other_codes, other_exps, other_degrees, tile_rows)
    panels = source.reshape(tiles_dev, tile_rows, row_width)
    target_tile = block_index[0, 0]
    source_tile = block_index[0, 1]
    own_blocks = adjacency[0]
    starting = jnp.zeros((dest_tiles, tile_rows, row_width), jnp.float32)
    piece = lax.all_gather(panels, "blk", axis=0, tiled=True)
    start = jnp.int32(0)
    piece_tiles = piece.shape[0]
    window = min(piece_tiles * dest_tiles, capacity)
    range_begin = jnp.sum((source_tile < start).astype(jnp.int32))
    range_end = jnp.sum((source_tile < start + piece_tiles).astype(jnp.int32))
    window_start = jnp.minimum(range_begin, capacity - window)
    picked = window_start + jnp.arange(window, dtype=jnp.int32)
    active = (picked >= range_begin) & (picked < range_end)
    offset_tiles = source_tile
    offset_tiles = jnp.clip(offset_tiles, 0, piece_tiles - 1)
    chosen = jnp.take(piece, offset_tiles, axis=0)
    products = jnp.einsum("kij,kjw->kiw", own_blocks, chosen, preferred_element_type=jnp.float32)
    placed = jnp.where(active, target_tile, dest_tiles)
    running = starting.at[placed].add(products, mode="drop")
    summed = lax.psum_scatter(
        running.reshape(groups, row_count, row_width), "grp", scatter_dimension=0, tiled=True
    )
    inverse = lax.rsqrt(degrees.astype(jnp.float32))
    return (summed * inverse[..., None]).astype(jnp.bfloat16)


def solution(mesh):
    placed = (
        P("side", ("grp", "blk"), None),
        P("side", ("grp", "blk")),
        P("side", ("grp", "blk")),
        P("side", ("grp", "blk"), None, None),
        P("side", None, ("grp", "blk")),
    )
    return jax.shard_map(
        shards,
        mesh=mesh,
        in_specs=placed,
        out_specs=P("side", ("grp", "blk"), None),
        check_vma=False,
    )
```

profile of v0, /device:TPU:2, one launch (start us, length us, event | category | flops | bytes accessed | tf_op | source)
XLA Modules:
  0.0 231.5 jit_solution(15946448544255334482)
XLA Ops:
  6.5 0.0 all-gather.2.cloned.1.call-start
  6.5 2.2 collective-permute-start
  8.8 0.0 collective-permute-start.2
  8.8 2.0 collective-permute-start.1
  10.8 1.9 collective-permute-done.1
  12.7 0.1 broadcast_bitcast_fusion
  12.7 0.0 collective-permute-done.2
  12.8 0.0 collective-permute-done
  12.8 0.9 multiply_convert_fusion.1
  13.6 0.0 all-gather.2.cloned.1.call-update
  13.7 0.0 reduce-scatter.2.cloned.1.call-start
  13.7 1.4 clamp_reduce_fusion
  15.7 2.0 fusion.11
  17.7 50.3 %all-gather.2.cloned.1.call-done = bf16[64,128,128]{2,1,0:T(8,128)(2,1)} async-done(((bf16[4,128,128]{2,1,0:T(8,128)(2,1)}), bf16[64,128,128]{2,1,0:T(8,128)(2,1)}) %all-gather.2.cloned.1.call-update) | async-done | bytes 2097168 | tf_op jit(solution)/shard_map/all_gather | solution.py:36
  68.1 12.9 %gather_fusion = bf16[384,128,128]{2,1,0:T(8,128)(2,1)} fusion(bf16[64,128,128]{2,1,0:T(8,128)(2,1)} %all-gather.2.cloned.1.call-done, s32[1024]{0:T(1024)S(1)} %pad_clamp_fusion), kind=kCustom, calls=%fused_computation | custom fusion | bytes 25167360 | tf_op jit(solution)/shard_map/jit(_take)/gather | solution.py:47
  81.0 22.7 %fusion.4 = f32[384,128,128]{1,2,0:T(8,128)} fusion(bf16[1,384,128,128]{3,2,1,0:T(8,128)(2,1)} %param.8, bf16[384,128,128]{2,1,0:T(8,128)(2,1)} %gather_fusion, pred[384]{0:T(512)(128)(4,1)S(1)} %compare_and_fusion), kind=kOutput, calls=%fused_computation.6 | convolution fusion | flops 1616904192 | bytes 50332032 | tf_op jit(solution)/shard_map/kij,kjw->kiw/dot_general | solution.py:48
  103.7 24.7 %copy.10 = f32[384,128,128]{2,1,0:T(8,128)} copy(f32[384,128,128]{1,2,0:T(8,128)} %fusion.4) | data formatting | bytes 50331648 | tf_op jit(solution)/shard_map/kij,kjw->kiw/dot_general | solution.py:48
  128.3 0.2 broadcast_in_dim.25
  128.6 0.0 copy-start.1
  128.6 50.2 %scatter_fusion = f32[32,128,128]{2,1,0:T(8,128)S(1)} fusion(f32[32,128,128]{2,1,0:T(8,128)S(1)} %broadcast_in_dim.25, s32[384]{0:T(512)S(1)} %get-tuple-element.9, f32[384,128,128]{2,1,0:T(8,128)} %copy.10), kind=kCustom, calls=%fused_computation.1 | custom fusion | flops 6291456 | bytes 75499008 | tf_op jit(solution)/shard_map/scatter-add | solution.py:50
  178.8 1.3 copy-done
  180.1 0.0 reduce-scatter.2.cloned.1.call-update
  180.2 42.7 %reduce-scatter.2.cloned.1.call-done = f32[1,512,128]{2,1,0:T(8,128)} async-done(((f32[8,512,128]{2,1,0:T(8,128)}), f32[1,512,128]{2,1,0:T(8,128)}) %reduce-scatter.2.cloned.1.call-update) | async-done | bytes 262160 | tf_op jit(solution)/shard_map/reduce_scatter | solution.py:51
  222.9 1.7 multiply_convert_fusion
  (7 shorter events, 0.0 us)
Async XLA Ops:
  6.5 61.5 %all-gather.2.cloned.1.call-start = ((), (), s32[]{:S(2)}) async-start(), calls=%async_computation.1 | async-start | bytes 2228224 | tf_op jit(solution)/shard_map/all_gather | solution.py:36
  6.5 6.2 %collective-permute-start = (bf16[1,512,128]{2,1,0:T(8,128)(2,1)}, bf16[1,512,128]{2,1,0:T(8,128)(2,1)S(1)}, u32[]{:S(2)}, u32[]{:S(2)}) collective-permute-start(bf16[1,512,128]{2,1,0:T(8,128)(2,1)} %param.5), channel_id=1, source_target_pairs={{0,128},{128,0},{1,129},{129,1},{2,130},{130,2},{3,131},{131,3},{4... | collective-permute-start | bytes 393224 | tf_op jit(solution)/shard_map/ppermute | solution.py:10
  8.8 4.0 %collective-permute-start.2 = (s32[1,512]{1,0:T(1,128)}, s32[1,512]{1,0:T(1,128)S(1)}, u32[]{:S(2)}, u32[]{:S(2)}) collective-permute-start(s32[1,512]{1,0:T(1,128)} %param.7), channel_id=1, source_target_pairs={{0,128},{128,0},{1,129},{129,1},{2,130},{130,2},{3,131},{131,3},{4... | collective-permute-start | bytes 6152 | tf_op jit(solution)/shard_map/ppermute | solution.py:10
  8.8 3.9 %collective-permute-start.1 = (s32[1,4]{1,0:T(1,128)}, s32[1,4]{1,0:T(1,128)S(1)}, u32[]{:S(2)}, u32[]{:S(2)}) collective-permute-start(s32[1,4]{1,0:T(1,128)} %param.6), channel_id=1, source_target_pairs={{0,128},{128,0},{1,129},{129,1},{2,130},{130,2},{3,131},{131,3},{4... | collective-permute-start | bytes 56 | tf_op jit(solution)/shard_map/ppermute | solution.py:10
  13.7 209.2 %reduce-scatter.2.cloned.1.call-start = ((), (), s32[]{:S(2)}) async-start(), calls=%async_computation.2 | async-start | bytes 2359296 | tf_op jit(solution)/shard_map/reduce_scatter | solution.py:51
  128.6 51.6 %copy-start.1 = (s32[1,512]{1,0:T(1,128)S(1)}, s32[1,512]{1,0:T(1,128)}, u32[]{:S(2)}) copy-start(s32[1,512]{1,0:T(1,128)} %param.7) | copy-start | bytes 6148
  178.8 1.4 copy-start
Sparse Core Ops, SparseCore 0:
  13.8 54.2 all-gather.1
  180.3 42.5 reduce-scatter.1
where the time goes:
time: 233 us; the launch traced here: 231 us
  waiting for transfers between devices  95 us (41%)
  other arithmetic  56.2 us (24%)
  local copies, waits for them, and re-layouts  39.2 us (17%)
  matrix products  22.7 us (10%)
  between operations  14.1 us (6%)
  starting transfers between devices  4.31 us (2%)
    all_gather x1, waiting for transfers between devices, shards(): piece = lax.all_gather(panels, 'blk', axis=0, tiled=True)  50.3 us
    scatter-add x1, other arithmetic, shards(): running = starting.at[placed].add(products, mode='drop')  50.2 us
    reduce_scatter x1, waiting for transfers between devices, shards(): lax.psum_scatter(running.reshape(groups, row_count, row_width), 'grp', sc...  42.7 us
    dot_general x1, local copies, waits for them, and re-layouts, shards(): jnp.einsum('kij,kjw->kiw', own_blocks, chosen, preferred_element_type=jnp...  24.7 us
    dot_general x1, matrix products, shards(): jnp.einsum('kij,kjw->kiw', own_blocks, chosen, preferred_element_type=jnp...  22.7 us
    gather x1, local copies, waits for them, and re-layouts, shards(): chosen = jnp.take(piece, offset_tiles, axis=0)  12.9 us
  transfers between devices with their start and end apart: 5, of which 3 were waited for; matrix products, arithmetic and copies ran while one was open for 2% of the time, Pallas kernels for 0%

commit v1 on v0

--- a/solution.py
+++ b/solution.py
@@ -33,7 +33,9 @@
     source_tile = block_index[0, 1]
     own_blocks = adjacency[0]
     starting = jnp.zeros((dest_tiles, tile_rows, row_width), jnp.float32)
-    piece = lax.all_gather(panels, "blk", axis=0, tiled=True)
+    piece = jnp.concatenate(
+        lax.all_to_all(jnp.stack([panels] * lax.axis_size("blk")), "blk", 0, 0), axis=0
+    )
     start = jnp.int32(0)
     piece_tiles = piece.shape[0]
     window = min(piece_tiles * dest_tiles, capacity)

time: 233 us -> 213 us (0.914)
  waiting for transfers between devices: 95 us -> 69.2 us
  starting transfers between devices: 4.31 us -> 10 us
    all_gather x1 -> x0, waiting for transfers between devices: 50.3 us -> none  [shards(): piece = lax.all_gather(panels, 'blk', axis=0, tiled=True)]
    all_to_all x0 -> x1, waiting for transfers between devices: none -> 25.3 us  [shards(): lax.all_to_all(jnp.stack([panels] * lax.axis_size('blk')), 'blk', 0, 0)]
    all_to_all x0 -> x1, starting transfers between devices: none -> 5.74 us  [shards(): lax.all_to_all(jnp.stack([panels] * lax.axis_size('blk')), 'blk', 0, 0)]
where the time goes in v1:
time: 213 us; the launch traced here: 211 us
  waiting for transfers between devices  69.2 us (32%)
  other arithmetic  55.6 us (26%)
  local copies, waits for them, and re-layouts  39.5 us (19%)
  matrix products  22.7 us (11%)
  between operations  14.1 us (7%)
  starting transfers between devices  10 us (5%)
    scatter-add x1, other arithmetic, shards(): running = starting.at[placed].add(products, mode='drop')  50.2 us
    reduce_scatter x1, waiting for transfers between devices, shards(): lax.psum_scatter(running.reshape(groups, row_count, row_width), 'grp', sc...  42.1 us
    all_to_all x1, waiting for transfers between devices, shards(): lax.all_to_all(jnp.stack([panels] * lax.axis_size('blk')), 'blk', 0, 0)  25.3 us
    dot_general x1, local copies, waits for them, and re-layouts, shards(): jnp.einsum('kij,kjw->kiw', own_blocks, chosen, preferred_element_type=jnp...  24.7 us
    dot_general x1, matrix products, shards(): jnp.einsum('kij,kjw->kiw', own_blocks, chosen, preferred_element_type=jnp...  22.7 us
    gather x1, local copies, waits for them, and re-layouts, shards(): chosen = jnp.take(piece, offset_tiles, axis=0)  11.3 us
    all_to_all x1, starting transfers between devices, shards(): lax.all_to_all(jnp.stack([panels] * lax.axis_size('blk')), 'blk', 0, 0)  5.74 us
    ppermute x3, starting transfers between devices, swapped(): return lax.ppermute(value, axis, pairs)  4.27 us
  transfers between devices with their start and end apart: 5, of which 3 were waited for; matrix products, arithmetic and copies ran while one was open for 2% of the time, Pallas kernels for 0%

profile of v1, /device:TPU:2, one launch (start us, length us, event | category | flops | bytes accessed | tf_op | source)
XLA Modules:
  0.0 211.1 jit_solution(1724848971624185353)
XLA Ops:
  6.5 2.2 %collective-permute-start = (bf16[1,512,128]{2,1,0:T(8,128)(2,1)}, bf16[1,512,128]{2,1,0:T(8,128)(2,1)S(1)}, u32[]{:S(2)}, u32[]{:S(2)}) collective-permute-start(bf16[1,512,128]{2,1,0:T(8,128)(2,1)} %param.5), channel_id=1, source_target_pairs={{0,128},{128,0},{1,129},{129,1},{2,130},{130,2},{3,131},{131,3},{4... | collective-permute-start | bytes 393224 | tf_op jit(solution)/shard_map/ppermute | solution.py:10
  8.8 0.0 collective-permute-start.2
  8.8 2.0 collective-permute-start.1
  10.8 1.9 collective-permute-done.1
  12.7 0.1 broadcast_bitcast_fusion
  12.7 0.0 collective-permute-done.2
  12.8 0.0 collective-permute-done
  12.8 0.2 multiply_convert_fusion.1
  13.0 1.9 stack.3
  14.8 5.7 %all-to-all-start = ((bf16[16,4,128,128]{3,2,1,0:T(8,128)(2,1)}), bf16[16,4,128,128]{3,2,1,0:T(8,128)(2,1)S(1)}, u32[]{:S(2)}, u32[]{:S(2)}) async-start(bf16[16,4,128,128]{3,2,1,0:T(8,128)(2,1)} %stack.3), calls=%async_computation | async-start | bytes 4194304 | tf_op jit(solution)/shard_map/all_to_all | solution.py:37
  20.6 0.0 reduce-scatter.2.cloned.1.call-start
  20.6 1.3 clamp_reduce_fusion
  22.6 2.0 fusion.11
  24.7 25.3 %all-to-all-done = bf16[16,4,128,128]{3,2,1,0:T(8,128)(2,1)S(1)} async-done(((bf16[16,4,128,128]{3,2,1,0:T(8,128)(2,1)}), bf16[16,4,128,128]{3,2,1,0:T(8,128)(2,1)S(1)}, u32[]{:S(2)}, u32[]{:S(2)}) %all-to-all-start) | async-done | bytes 2097184 | tf_op jit(solution)/shard_map/all_to_all | solution.py:37
  50.0 11.3 %gather_fusion = bf16[384,128,128]{2,1,0:T(8,128)(2,1)} fusion(bf16[64,128,128]{2,1,0:T(8,128)(2,1)S(1)} %bitcast.23, s32[1024]{0:T(1024)S(1)} %pad_clamp_fusion), kind=kCustom, calls=%fused_computation | custom fusion | bytes 25167360 | tf_op jit(solution)/shard_map/jit(_take)/gather | solution.py:49
  61.3 22.7 %fusion.4 = f32[384,128,128]{1,2,0:T(8,128)} fusion(bf16[1,384,128,128]{3,2,1,0:T(8,128)(2,1)} %param.8, bf16[384,128,128]{2,1,0:T(8,128)(2,1)} %gather_fusion, pred[384]{0:T(512)(128)(4,1)S(1)} %compare_and_fusion), kind=kOutput, calls=%fused_computation.6 | convolution fusion | flops 1616904192 | bytes 50332032 | tf_op jit(solution)/shard_map/kij,kjw->kiw/dot_general | solution.py:50
  84.0 24.7 %copy.8 = f32[384,128,128]{2,1,0:T(8,128)} copy(f32[384,128,128]{1,2,0:T(8,128)} %fusion.4) | data formatting | bytes 50331648 | tf_op jit(solution)/shard_map/kij,kjw->kiw/dot_general | solution.py:50
  108.6 0.2 broadcast_in_dim.25
  108.9 0.0 copy-start.1
  108.9 50.2 %scatter_fusion = f32[32,128,128]{2,1,0:T(8,128)S(1)} fusion(f32[32,128,128]{2,1,0:T(8,128)S(1)} %broadcast_in_dim.25, s32[384]{0:T(512)S(1)} %get-tuple-element.9, f32[384,128,128]{2,1,0:T(8,128)} %copy.8), kind=kCustom, calls=%fused_computation.1 | custom fusion | flops 6291456 | bytes 75499008 | tf_op jit(solution)/shard_map/scatter-add | solution.py:52
  159.1 1.3 copy-done
  160.4 0.0 reduce-scatter.2.cloned.1.call-update
  160.5 42.1 %reduce-scatter.2.cloned.1.call-done = f32[1,512,128]{2,1,0:T(8,128)} async-done(((f32[8,512,128]{2,1,0:T(8,128)}), f32[1,512,128]{2,1,0:T(8,128)}) %reduce-scatter.2.cloned.1.call-update) | async-done | bytes 262160 | tf_op jit(solution)/shard_map/reduce_scatter | solution.py:53
  202.6 1.7 multiply_convert_fusion
  (7 shorter events, 0.0 us)
Async XLA Ops:
  6.5 6.2 %collective-permute-start = (bf16[1,512,128]{2,1,0:T(8,128)(2,1)}, bf16[1,512,128]{2,1,0:T(8,128)(2,1)S(1)}, u32[]{:S(2)}, u32[]{:S(2)}) collective-permute-start(bf16[1,512,128]{2,1,0:T(8,128)(2,1)} %param.5), channel_id=1, source_target_pairs={{0,128},{128,0},{1,129},{129,1},{2,130},{130,2},{3,131},{131,3},{4... | collective-permute-start | bytes 393224 | tf_op jit(solution)/shard_map/ppermute | solution.py:10
  8.8 4.0 %collective-permute-start.2 = (s32[1,512]{1,0:T(1,128)}, s32[1,512]{1,0:T(1,128)S(1)}, u32[]{:S(2)}, u32[]{:S(2)}) collective-permute-start(s32[1,512]{1,0:T(1,128)} %param.7), channel_id=1, source_target_pairs={{0,128},{128,0},{1,129},{129,1},{2,130},{130,2},{3,131},{131,3},{4... | collective-permute-start | bytes 6152 | tf_op jit(solution)/shard_map/ppermute | solution.py:10
  8.8 3.9 %collective-permute-start.1 = (s32[1,4]{1,0:T(1,128)}, s32[1,4]{1,0:T(1,128)S(1)}, u32[]{:S(2)}, u32[]{:S(2)}) collective-permute-start(s32[1,4]{1,0:T(1,128)} %param.6), channel_id=1, source_target_pairs={{0,128},{128,0},{1,129},{129,1},{2,130},{130,2},{3,131},{131,3},{4... | collective-permute-start | bytes 56 | tf_op jit(solution)/shard_map/ppermute | solution.py:10
  14.8 35.1 %all-to-all-start = ((bf16[16,4,128,128]{3,2,1,0:T(8,128)(2,1)}), bf16[16,4,128,128]{3,2,1,0:T(8,128)(2,1)S(1)}, u32[]{:S(2)}, u32[]{:S(2)}) async-start(bf16[16,4,128,128]{3,2,1,0:T(8,128)(2,1)} %stack.3), calls=%async_computation | async-start | bytes 4194304 | tf_op jit(solution)/shard_map/all_to_all | solution.py:37
  20.6 182.0 %reduce-scatter.2.cloned.1.call-start = ((), (), s32[]{:S(2)}) async-start(), calls=%async_computation.2 | async-start | bytes 2359296 | tf_op jit(solution)/shard_map/reduce_scatter | solution.py:53
  108.9 51.6 %copy-start.1 = (s32[1,512]{1,0:T(1,128)S(1)}, s32[1,512]{1,0:T(1,128)}, u32[]{:S(2)}) copy-start(s32[1,512]{1,0:T(1,128)} %param.7) | copy-start | bytes 6148
  159.1 1.4 copy-start
Sparse Core Ops, SparseCore 0:
  160.6 41.9 reduce-scatter.1
